TPU v7x, 32 devices: a whole 2x2x4 slice. The times are simulated.
32 devices in a mesh: regions: 2 (over y), gz: 8 (over z, x), gy: 2 (over core).
Axes of the slice: x: 2, y: 2, z: 4, core: 2. Of those that a mesh axis runs over, the one named last changes fastest.
Arguments:
- iterate: float32 [16, 32, 128, 256], P(None, ('regions', 'gz'), 'gy'), parts along dimension 1, may hold values from -6 to 6
- residual: float32 [16, 32, 128, 256], P(None, ('regions', 'gz'), 'gy'), parts along dimension 1, may hold values from -16 to 16
- labels: int32 [32, 128, 256], P(('regions', 'gz'), 'gy'), parts along dimension 0, may hold values from 0 to 7
- boundary: int32 [32, 128, 256], P(('regions', 'gz'), 'gy'), parts along dimension 0, may hold values 0 or 1
Outputs:
- iterate_out: float32 [16, 32, 128, 256], P(None, ('regions', 'gz'), 'gy'), parts along dimension 1
- residual_out: float32 [16, 32, 128, 256], P(None, ('regions', 'gz'), 'gy'), parts along dimension 1
There are 2 independent parts, one for each index of `regions`. A program takes and returns all parts, laid end to end along the dimension named above; each array names one. Nothing has to cross between parts.
All inputs are finite; a program needn't handle non-finite values. No bound on the sum of `boundary` on one device may be relied on, other than what follows from the above.
Results may differ from a plain program's by a relative error of at most 0.0003.
Values sent between devices are 32-bit elements; how exact they have to be, the bound alone decides.
A program may use at most 128 MiB of HBM per device.

v0:
```python
import math

import jax
import jax.numpy as jnp
from jax import lax
from jax.sharding import PartitionSpec as P

NCLASS = 8
ITERS = 3


contrast_log = 4.0 * math.log(10.0)
highest = lax.Precision.HIGHEST


def extended_2(cells, sides, width):
    for axis, dim in sides:
        count = lax.axis_size(axis)
        ends = count - 1
        head = lax.slice_in_dim(cells, 0, width, axis=dim)
        tail = lax.slice_in_dim(cells, cells.shape[dim] - width, cells.shape[dim], axis=dim)
        cells = jnp.concatenate(
            [
                lax.ppermute(tail, axis, [(i, (i + 1) % count) for i in range(ends)]),
                cells,
                lax.ppermute(head, axis, [((i + 1) % count, i) for i in range(ends)]),
            ],
            axis=dim,
        )
    return cells


def shift_cells(block, forward):
    widths = [(0, 0)] * (block.ndim - 1)
    if forward:
        return jnp.pad(block[..., 1:], widths + [(0, 1)])
    return jnp.pad(block[..., :-1], widths + [(1, 0)])


def neighbors(extended):
    center = extended[..., 1:-1, 1:-1, :]
    beside = [
        extended[..., 2:, 1:-1, :],
        extended[..., :-2, 1:-1, :],
        extended[..., 1:-1, 2:, :],
        extended[..., 1:-1, :-2, :],
        shift_cells(center, True),
        shift_cells(center, False),
    ]
    return (center, beside)


def couplings_of(extended):
    coef_center, coef_beside = neighbors(extended[0])
    inner_center, inner_beside = neighbors(extended[1])
    diagonal = jnp.zeros_like(coef_center)
    offsets = []
    for neighbor_coef, neighbor_inner in zip(coef_beside, inner_beside):
        face_coef = jnp.where(
            neighbor_coef > 0.0,
            2.0 * coef_center * neighbor_coef / (coef_center + neighbor_coef),
            coef_center,
        )
        diagonal = diagonal + face_coef
        offsets.append(inner_center * face_coef * neighbor_inner)
    diagonal = inner_center * diagonal + (1.0 - inner_center)
    return (diagonal, offsets)


def apply_operator(diagonal, offsets, extended):
    center, beside = neighbors(extended)
    coupled = offsets[0] * beside[0]
    for weight, values in zip(offsets[1:], beside[1:]):
        coupled = coupled + weight * values
    return diagonal * center - coupled


def cell_fields(labels, boundary):
    coef = jnp.exp(labels.astype(jnp.float32) * (contrast_log / (NCLASS - 1)))
    interior = (1 - boundary).astype(jnp.float32)
    return jnp.stack([coef, interior])


def gram(left_block, right_block):
    left_flat = left_block.reshape(left_block.shape[0], -1)
    right_flat = right_block.reshape(right_block.shape[0], -1)
    return lax.dot_general(left_flat, right_flat, (((1,), (1,)), ((), ())), precision=highest)


def combine(block, weights):
    flat = block.reshape(block.shape[0], -1)
    mixed = lax.dot_general(weights, flat, (((0,), (0,)), ((), ())), precision=highest)
    return mixed.reshape(block.shape)


def spd_solve(matrix, right):
    factor = jnp.linalg.cholesky(matrix)
    return jax.scipy.linalg.cho_solve((factor, True), right)


def direction_cells(field):
    return extended_2(field, (("gz", 1), ("gy", 2)), 1)


def on_device(iterate, residual, labels, boundary):
    fields = cell_fields(labels, boundary)
    extended = extended_2(fields, (("gz", 1), ("gy", 2)), 1)
    diagonal, offsets = couplings_of(extended)
    inverse_diag = 1.0 / diagonal
    scaled = inverse_diag * residual
    direction = scaled
    for iteration in range(ITERS):
        direction_ext = direction_cells(direction)
        image = apply_operator(diagonal, offsets, direction_ext)
        weighted = inverse_diag * image
        summed_rho, curvature, cross_gram, image_gram = lax.psum(
            (
                gram(residual, scaled),
                gram(direction, image),
                gram(scaled, image),
                gram(image, weighted),
            ),
            ("gz", "gy"),
        )
        step_size = spd_solve(curvature, summed_rho)
        iterate = iterate + combine(direction, step_size)
        residual = residual - combine(image, step_size)
        if iteration + 1 < ITERS:
            scaled = inverse_diag * residual
            moved = jnp.dot(cross_gram, step_size, precision=highest)
            quadratic = jnp.dot(
                step_size.T, jnp.dot(image_gram, step_size, precision=highest), precision=highest
            )
            next_rho = summed_rho - moved - moved.T + quadratic
            momentum = spd_solve(summed_rho, next_rho)
            direction = scaled + combine(direction, momentum)
            summed_rho = next_rho
    return (iterate, residual)


def solution(mesh):
    placed = (
        P(None, ("regions", "gz"), "gy", None),
        P(None, ("regions", "gz"), "gy", None),
        P(("regions", "gz"), "gy", None),
        P(("regions", "gz"), "gy", None),
    )
    return jax.shard_map(
        on_device,
        mesh=mesh,
        in_specs=placed,
        out_specs=(P(None, ("regions", "gz"), "gy", None), P(None, ("regions", "gz"), "gy", None)),
        check_vma=False,
    )
```

profile of v0, /device:TPU:0, one launch (start us, length us, event | category | flops | bytes accessed | tf_op | source)
XLA Modules:
  0.0 462.8 jit_solution(4175048000201397154)
XLA Ops:
  3.8 5.5 %collective-permute-start = (f32[2,1,64,256]{3,2,1,0:T(8,128)S(1)}, f32[2,1,64,256]{3,2,1,0:T(8,128)S(1)}, u32[]{:S(2)}, u32[]{:S(2)}) collective-permute-start(f32[2,1,64,256]{3,2,1,0:T(8,128)S(1)} %get-tuple-element.51), channel_id=1, source_target_pairs={{0,2},{2,4},{4,6},{6,8},{8,10},{10,12},{12,14},{1,3},{3,5},{5,7},{... | collective-permute-start | bytes 393224 | tf_op jit(solution)/shard_map/ppermute | solution.py:24
  23.4 5.1 %collective-permute-start.5 = (f32[16,1,64,256]{3,0,2,1:T(8,128)S(1)}, f32[16,1,64,256]{3,0,2,1:T(8,128)S(1)}, u32[]{:S(2)}, u32[]{:S(2)}) collective-permute-start(f32[16,1,64,256]{3,0,2,1:T(8,128)S(1)} %get-tuple-element.35), channel_id=1, source_target_pairs={{0,2},{2,4},{4,6},{6,8},{8,10},{10,12},{12,14},{1,3},{3,5},{5,7},{... | collective-permute-start | bytes 3145736 | tf_op jit(solution)/shard_map/ppermute | solution.py:24
  28.5 3.5 fusion.74
  32.7 17.4 %collective-permute-done.4 = f32[16,1,64,256]{3,0,2,1:T(8,128)S(1)} collective-permute-done((f32[16,1,64,256]{3,0,2,1:T(8,128)S(1)}, f32[16,1,64,256]{3,0,2,1:T(8,128)S(1)}, u32[]{:S(2)}, u32[]{:S(2)}) %collective-permute-start.4) | collective-permute-done | bytes 1048608 | tf_op jit(solution)/shard_map/ppermute | solution.py:26
  50.1 22.6 %collective-permute-done.5 = f32[16,1,64,256]{3,0,2,1:T(8,128)S(1)} collective-permute-done((f32[16,1,64,256]{3,0,2,1:T(8,128)S(1)}, f32[16,1,64,256]{3,0,2,1:T(8,128)S(1)}, u32[]{:S(2)}, u32[]{:S(2)}) %collective-permute-start.5) | collective-permute-done | bytes 1048608 | tf_op jit(solution)/shard_map/ppermute | solution.py:24
  79.0 3.2 fusion.34
  82.2 3.8 convolution_bitcast_fusion.5
  91.3 60.9 %all-reduce.12 = (f32[16,16]{0,1:T(8,128)S(1)}, f32[16,16]{0,1:T(8,128)S(1)}, f32[16,16]{1,0:T(8,128)S(1)}) all-reduce(f32[16,16]{0,1:T(8,128)S(1)} %fusion.74, f32[16,16]{0,1:T(8,128)S(1)} %convolution_bitcast_fusion.5, f32[16,16]{1,0:T(8,128)S(1)} %fusion.86), channel_id=1, replica_groups=mesh['regions'=2,'gz'=8,'gy'=2] {'gz','gy'}, use_global_device_ids=true, to_apply=%region_3.5 | all-reduce | flops 768 | bytes 6144 | tf_op jit(solution)/shard_map/psum | solution.py:116
  157.0 6.3 %copy_subtract_fusion = f32[16,2,64,256]{3,0,2,1:T(8,128)S(1)} fusion(f32[16,2,64,256]{3,2,1,0:T(8,128)} %param.8, f32[2,64,256,16]{2,1,0,3:T(8,128)} %bitcast.241, f32[16,16]{1,0:T(8,128)S(1)} %fusion.124), kind=kOutput, calls=%fused_computation.85 | convolution fusion | flops 101187584 | bytes 6292480 | tf_op jit(solution)/shard_map/dot_general | solution.py:92
  168.1 4.5 multiply_add_fusion.1
  174.1 4.6 collective-permute-start.9
  179.5 15.8 %collective-permute-done.8 = f32[16,1,64,256]{3,0,2,1:T(8,128)S(1)} collective-permute-done((f32[16,1,64,256]{3,0,2,1:T(8,128)S(1)}, f32[16,1,64,256]{3,0,2,1:T(8,128)S(1)}, u32[]{:S(2)}, u32[]{:S(2)}) %collective-permute-start.8) | collective-permute-done | bytes 1048608 | tf_op jit(solution)/shard_map/ppermute | solution.py:26
  195.3 18.0 %collective-permute-done.9 = f32[16,1,64,256]{3,0,2,1:T(8,128)S(1)} collective-permute-done((f32[16,1,64,256]{3,0,2,1:T(8,128)S(1)}, f32[16,1,64,256]{3,0,2,1:T(8,128)S(1)}, u32[]{:S(2)}, u32[]{:S(2)}) %collective-permute-start.9) | collective-permute-done | bytes 1048608 | tf_op jit(solution)/shard_map/ppermute | solution.py:24
  222.3 3.2 fusion.24
  236.6 62.6 %all-reduce.11 = (f32[16,16]{0,1:T(8,128)S(1)}, f32[16,16]{0,1:T(8,128)S(1)}, f32[16,16]{1,0:T(8,128)S(1)}, f32[16,16]{1,0:T(8,128)S(1)}) all-reduce(f32[16,16]{0,1:T(8,128)S(1)} %fusion.77, f32[16,16]{0,1:T(8,128)S(1)} %convolution_bitcast_fusion.3, f32[16,16]{1,0:T(8,128)S(1)} %fusion.89, ...), channel_id=1, replica_groups=mesh['regions'=2,'gz'=8,'gy'=2] {'gz','gy'}, use_global_device_ids=true, to_apply=%region_6.9 | all-reduce | flops 1024 | bytes 8192 | tf_op jit(solution)/shard_map/psum | solution.py:116
  303.5 5.7 %fusion.68 = f32[16,2,64,256]{3,0,2,1:T(8,128)} fusion(f32[16,2,64,256]{3,0,2,1:T(8,128)S(1)} %copy_subtract_fusion, f32[2,64,256,16]{2,1,0,3:T(8,128)} %bitcast.240, f32[16,16]{1,0:T(8,128)S(1)} %fusion.113), kind=kOutput, calls=%fused_computation.89 | convolution fusion | flops 101187584 | bytes 6292480 | tf_op jit(solution)/shard_map/dot_general | solution.py:92
  314.1 5.2 %multiply_add_fusion = f32[16,2,64,256]{3,0,2,1:T(8,128)S(1)} fusion(f32[16,2,64,256]{3,0,2,1:T(8,128)} %fusion.68, f32[16,16,1,1]{0,1,3,2:T(8,128)S(1)} %convolution_bitcast_fusion.2, f32[2,64,256,16]{2,1,0,3:T(8,128)} %bitcast.234, f32[2,64,256]{2,1,0:T(8,128)S(1)} %get-tuple-element.17), kind=kOutput, calls=%fused_computation.6 | convolution fusion | flops 101711872 | bytes 6423552 | tf_op jit(solution)/shard_map/dot_general | solution.py:92
  320.9 4.6 collective-permute-start.13
  325.6 4.2 fusion.52
  330.5 11.6 %collective-permute-done.12 = f32[16,1,64,256]{3,0,2,1:T(8,128)S(1)} collective-permute-done((f32[16,1,64,256]{3,0,2,1:T(8,128)S(1)}, f32[16,1,64,256]{3,0,2,1:T(8,128)S(1)}, u32[]{:S(2)}, u32[]{:S(2)}) %collective-permute-start.12) | collective-permute-done | bytes 1048608 | tf_op jit(solution)/shard_map/ppermute | solution.py:26
  342.1 18.0 %collective-permute-done.13 = f32[16,1,64,256]{3,0,2,1:T(8,128)S(1)} collective-permute-done((f32[16,1,64,256]{3,0,2,1:T(8,128)S(1)}, f32[16,1,64,256]{3,0,2,1:T(8,128)S(1)}, u32[]{:S(2)}, u32[]{:S(2)}) %collective-permute-start.13) | collective-permute-done | bytes 1048608 | tf_op jit(solution)/shard_map/ppermute | solution.py:24
  376.0 62.5 %all-reduce.10 = (f32[16,16]{1,0:T(8,128)S(1)}, f32[16,16]{0,1:T(8,128)S(1)}) all-reduce(f32[16,16]{1,0:T(8,128)S(1)} %fusion.83, f32[16,16]{0,1:T(8,128)S(1)} %convolution_bitcast_fusion.1), channel_id=1, replica_groups=mesh['regions'=2,'gz'=8,'gy'=2] {'gz','gy'}, use_global_device_ids=true, to_apply=%region_10.13 | all-reduce | flops 512 | bytes 4096 | tf_op jit(solution)/shard_map/psum | solution.py:116
  442.9 4.5 fusion.42
  447.5 5.7 %fusion.49 = f32[16,2,64,256]{3,0,2,1:T(8,128)S(1)} fusion(f32[16,2,64,256]{3,0,2,1:T(8,128)S(1)} %fusion.42, f32[16,2,64,256]{3,0,2,1:T(8,128)S(1)} %copy-done.6, f32[16,2,64,256]{3,2,1,0:T(8,128)} %param.7, f32[2,64,256,16]{2,1,0,3:T(8,128)S(1)} %bitcast.237, f32[16,16]{1,0:T(8,128)S(1)} %fusion.124), kind=kOutput, calls=%fused_computation.76 | convolution fusion | flops 102236160 | bytes 10486784 | tf_op jit(solution)/shard_map/dot_general | solution.py:92
  (125 shorter events, 102.4 us)
Async XLA Ops:
  2.5 8.4 %collective-permute-start.1 = (f32[2,1,64,256]{3,2,1,0:T(8,128)S(1)}, f32[2,1,64,256]{3,2,1,0:T(8,128)S(1)}, u32[]{:S(2)}, u32[]{:S(2)}) collective-permute-start(f32[2,1,64,256]{3,2,1,0:T(8,128)S(1)} %get-tuple-element.52), channel_id=1, source_target_pairs={{2,0},{4,2},{6,4},{8,6},{10,8},{12,10},{14,12},{3,1},{5,3},{7,5},{... | collective-permute-start | bytes 393224 | tf_op jit(solution)/shard_map/ppermute | solution.py:26
  3.8 10.0 %collective-permute-start = (f32[2,1,64,256]{3,2,1,0:T(8,128)S(1)}, f32[2,1,64,256]{3,2,1,0:T(8,128)S(1)}, u32[]{:S(2)}, u32[]{:S(2)}) collective-permute-start(f32[2,1,64,256]{3,2,1,0:T(8,128)S(1)} %get-tuple-element.51), channel_id=1, source_target_pairs={{0,2},{2,4},{4,6},{6,8},{8,10},{10,12},{12,14},{1,3},{3,5},{5,7},{... | collective-permute-start | bytes 393224 | tf_op jit(solution)/shard_map/ppermute | solution.py:24
  13.9 4.3 collective-permute-start.3
  15.2 3.8 collective-permute-start.2
  19.1 1.6 copy-start
  22.1 28.1 %collective-permute-start.4 = (f32[16,1,64,256]{3,0,2,1:T(8,128)S(1)}, f32[16,1,64,256]{3,0,2,1:T(8,128)S(1)}, u32[]{:S(2)}, u32[]{:S(2)}) collective-permute-start(f32[16,1,64,256]{3,0,2,1:T(8,128)S(1)} %get-tuple-element.36), channel_id=1, source_target_pairs={{2,0},{4,2},{6,4},{8,6},{10,8},{12,10},{14,12},{3,1},{5,3},{7,5},{... | collective-permute-start | bytes 3145736 | tf_op jit(solution)/shard_map/ppermute | solution.py:26
  23.4 49.4 %collective-permute-start.5 = (f32[16,1,64,256]{3,0,2,1:T(8,128)S(1)}, f32[16,1,64,256]{3,0,2,1:T(8,128)S(1)}, u32[]{:S(2)}, u32[]{:S(2)}) collective-permute-start(f32[16,1,64,256]{3,0,2,1:T(8,128)S(1)} %get-tuple-element.35), channel_id=1, source_target_pairs={{0,2},{2,4},{4,6},{6,8},{8,10},{10,12},{12,14},{1,3},{3,5},{5,7},{... | collective-permute-start | bytes 3145736 | tf_op jit(solution)/shard_map/ppermute | solution.py:24
  72.8 6.2 %collective-permute-start.7 = (f32[16,4,1,256]{3,0,2,1:T(8,128)S(1)}, f32[16,4,1,256]{3,0,2,1:T(8,128)S(1)}, u32[]{:S(2)}, u32[]{:S(2)}) collective-permute-start(f32[16,4,1,256]{3,0,2,1:T(8,128)S(1)} %get-tuple-element.24), channel_id=1, source_target_pairs={{0,1},{2,3},{4,5},{6,7},{8,9},{10,11},{12,13},{14,15},{16,17},{18,... | collective-permute-start | bytes 196616 | tf_op jit(solution)/shard_map/ppermute | solution.py:24
  74.7 4.3 collective-permute-start.6
  172.8 22.4 %collective-permute-start.8 = (f32[16,1,64,256]{3,0,2,1:T(8,128)S(1)}, f32[16,1,64,256]{3,0,2,1:T(8,128)S(1)}, u32[]{:S(2)}, u32[]{:S(2)}) collective-permute-start(f32[16,1,64,256]{3,0,2,1:T(8,128)S(1)} %get-tuple-element.32), channel_id=1, source_target_pairs={{2,0},{4,2},{6,4},{8,6},{10,8},{12,10},{14,12},{3,1},{5,3},{7,5},{... | collective-permute-start | bytes 3145736 | tf_op jit(solution)/shard_map/ppermute | solution.py:26
  174.1 39.1 %collective-permute-start.9 = (f32[16,1,64,256]{3,0,2,1:T(8,128)S(1)}, f32[16,1,64,256]{3,0,2,1:T(8,128)S(1)}, u32[]{:S(2)}, u32[]{:S(2)}) collective-permute-start(f32[16,1,64,256]{3,0,2,1:T(8,128)S(1)} %get-tuple-element.31), channel_id=1, source_target_pairs={{0,2},{2,4},{4,6},{6,8},{8,10},{10,12},{12,14},{1,3},{3,5},{5,7},{... | collective-permute-start | bytes 3145736 | tf_op jit(solution)/shard_map/ppermute | solution.py:24
  213.2 9.0 %collective-permute-start.11 = (f32[16,4,1,256]{3,0,2,1:T(8,128)S(1)}, f32[16,4,1,256]{3,0,2,1:T(8,128)S(1)}, u32[]{:S(2)}, u32[]{:S(2)}) collective-permute-start(f32[16,4,1,256]{3,0,2,1:T(8,128)S(1)} %get-tuple-element.22), channel_id=1, source_target_pairs={{0,1},{2,3},{4,5},{6,7},{8,9},{10,11},{12,13},{14,15},{16,17},{18,... | collective-permute-start | bytes 196616 | tf_op jit(solution)/shard_map/ppermute | solution.py:24
  215.2 7.1 %collective-permute-start.10 = (f32[16,4,1,256]{3,0,2,1:T(8,128)S(1)}, f32[16,4,1,256]{3,0,2,1:T(8,128)S(1)}, u32[]{:S(2)}, u32[]{:S(2)}) collective-permute-start(f32[16,4,1,256]{3,0,2,1:T(8,128)S(1)} %get-tuple-element.21), channel_id=1, source_target_pairs={{1,0},{3,2},{5,4},{7,6},{9,8},{11,10},{13,12},{15,14},{17,16},{19,... | collective-permute-start | bytes 196616 | tf_op jit(solution)/shard_map/ppermute | solution.py:26
  319.3 6.2 %copy-start.2 = (f32[2,8,128,256]{3,2,1,0:T(8,128)S(1)}, f32[2,8,128,256]{3,2,1,0:T(8,128)}, u32[]{:S(2)}) copy-start(f32[2,8,128,256]{3,2,1,0:T(8,128)} %copy.97) | copy-start | bytes 6291460
  319.5 22.6 %collective-permute-start.12 = (f32[16,1,64,256]{3,0,2,1:T(8,128)S(1)}, f32[16,1,64,256]{3,0,2,1:T(8,128)S(1)}, u32[]{:S(2)}, u32[]{:S(2)}) collective-permute-start(f32[16,1,64,256]{3,0,2,1:T(8,128)S(1)} %get-tuple-element.28), channel_id=1, source_target_pairs={{2,0},{4,2},{6,4},{8,6},{10,8},{12,10},{14,12},{3,1},{5,3},{7,5},{... | collective-permute-start | bytes 3145736 | tf_op jit(solution)/shard_map/ppermute | solution.py:26
  320.9 39.1 %collective-permute-start.13 = (f32[16,1,64,256]{3,0,2,1:T(8,128)S(1)}, f32[16,1,64,256]{3,0,2,1:T(8,128)S(1)}, u32[]{:S(2)}, u32[]{:S(2)}) collective-permute-start(f32[16,1,64,256]{3,0,2,1:T(8,128)S(1)} %get-tuple-element.27), channel_id=1, source_target_pairs={{0,2},{2,4},{4,6},{6,8},{8,10},{10,12},{12,14},{1,3},{3,5},{5,7},{... | collective-permute-start | bytes 3145736 | tf_op jit(solution)/shard_map/ppermute | solution.py:24
  330.5 32.8 %copy-start.1 = (f32[16,2,64,256]{3,0,2,1:T(8,128)S(1)}, f32[16,2,64,256]{3,0,2,1:T(8,128)}, u32[]{:S(2)}) copy-start(f32[16,2,64,256]{3,0,2,1:T(8,128)} %fusion.68) | copy-start | bytes 6291460
  360.0 8.5 %collective-permute-start.15 = (f32[16,4,1,256]{3,0,2,1:T(8,128)S(1)}, f32[16,4,1,256]{3,0,2,1:T(8,128)S(1)}, u32[]{:S(2)}, u32[]{:S(2)}) collective-permute-start(f32[16,4,1,256]{3,0,2,1:T(8,128)S(1)} %get-tuple-element.20), channel_id=1, source_target_pairs={{0,1},{2,3},{4,5},{6,7},{8,9},{10,11},{12,13},{14,15},{16,17},{18,... | collective-permute-start | bytes 196616 | tf_op jit(solution)/shard_map/ppermute | solution.py:24
  362.0 6.6 %collective-permute-start.14 = (f32[16,4,1,256]{3,0,2,1:T(8,128)S(1)}, f32[16,4,1,256]{3,0,2,1:T(8,128)S(1)}, u32[]{:S(2)}, u32[]{:S(2)}) collective-permute-start(f32[16,4,1,256]{3,0,2,1:T(8,128)S(1)} %get-tuple-element.19), channel_id=1, source_target_pairs={{1,0},{3,2},{5,4},{7,6},{9,8},{11,10},{13,12},{15,14},{17,16},{19,... | collective-permute-start | bytes 196616 | tf_op jit(solution)/shard_map/ppermute | solution.py:26
  371.8 1.3 copy-start.4
  442.9 4.6 copy-start.3
  442.9 4.6 copy-start.6
  453.2 2.5 copy-start.5
where the time goes:
time: 469 us; the launch traced here: 463 us
  blocking collectives  186 us (40%)
  waiting for transfers between devices  109 us (23%)
  matrix products  68.6 us (15%)
  starting transfers between devices  39.8 us (8%)
  other arithmetic  33.3 us (7%)
  local copies, waits for them, and re-layouts  24.9 us (5%)
    psum x3, blocking collectives, on_device(): lax.psum((gram(residual, scaled), gram(direction, image), gram(scaled, im...  186 us
    ppermute x8, waiting for transfers between devices, extended_2(): lax.ppermute(tail, axis, [(i, (i + 1) % count) for i in range(ends)])  62.3 us
    ppermute x8, waiting for transfers between devices, extended_2(): lax.ppermute(head, axis, [((i + 1) % count, i) for i in range(ends)])  46.3 us
    dot_general x8, matrix products, combine(): lax.dot_general(weights, flat, (((0,), (0,)), ((), ())), precision=highest)  38.9 us
    ppermute x8, starting transfers between devices, extended_2(): lax.ppermute(tail, axis, [(i, (i + 1) % count) for i in range(ends)])  28.6 us
    dot_general x9, matrix products, gram(): lax.dot_general(left_flat, right_flat, (((1,), (1,)), ((), ())), precisio...  26.8 us
    unnamed x22, local copies, waits for them, and re-layouts  21.5 us
    ppermute x8, starting transfers between devices, extended_2(): lax.ppermute(head, axis, [((i + 1) % count, i) for i in range(ends)])  11.1 us
  transfers between devices with their start and end apart: 16, of which 9 were waited for; matrix products, arithmetic and copies ran while one was open for 5% of the time, Pallas kernels for 0%

commit v1 on v0

v1 whole, which is shorter than its diff:
```python
import functools
import math

import jax
import jax.numpy as jnp
from jax import lax
from jax.experimental import pallas as pl
from jax.experimental.pallas import tpu as pltpu
from jax.sharding import PartitionSpec as P

NCLASS = 8
ITERS = 3
DEPTH = ITERS
YH = 4
OFF = YH + 1
LH = 8
SHIFT = LH - OFF
GROUP = 4
REDUCES = 2 * ITERS - 1

contrast_log = 4.0 * math.log(10.0)
MESH = pl.DeviceIdType.MESH
F32 = jnp.float32
BF16 = jnp.bfloat16


def split(value):
    high = value.astype(BF16)
    return high, (value - high.astype(F32)).astype(BF16)


def dot_nt(left, right):
    return lax.dot_general(left, right, (((1,), (1,)), ((), ())), preferred_element_type=F32)


def exact(left, right, contract):
    parts = []
    for value in (left, right):
        first, rest = split(value)
        third = (value - first.astype(F32) - rest.astype(F32)).astype(BF16)
        parts.append((first, rest, third))
    result = None
    for i, j in ((2, 0), (1, 1), (0, 2), (1, 0), (0, 1), (0, 0)):
        term = lax.dot_general(parts[0][i], parts[1][j], (contract, ((), ())), preferred_element_type=F32)
        result = term if result is None else result + term
    return result


def exact_nt(left, right):
    return exact(left, right, ((1,), (1,)))


def exact_nn(left, right):
    return exact(left, right, ((1,), (0,)))


def eliminate(matrix):
    m = matrix.shape[0]
    row_id = lax.broadcasted_iota(jnp.int32, matrix.shape, 0)
    for k in range(m):
        pivot_row = matrix[k : k + 1, :] / matrix[k : k + 1, k : k + 1]
        matrix = jnp.where(row_id == k, pivot_row, matrix - matrix[:, k : k + 1] * pivot_row)
    return matrix


def kernel(
    sizes,
    iterate, residual, labels, boundary, iterate_out, residual_out,
    X, R, D, IM, LAB, BND, COEF, INNER, INV, DIAG, WZU, WZD, WYU, WYD, WXR, WXL,
    acc, gsend, gslots, wbuf,
    local_sem, bulk_send, bulk_recv, strip_send, strip_recv, gram_send, gram_recv, out_sem,
):
    gz_count, gy_count, m, nz, ny, nx = sizes
    total = gz_count * gy_count
    region = lax.axis_index("regions")
    gz = lax.axis_index("gz")
    gy = lax.axis_index("gy")
    me = gz * gy_count + gy
    rows_window = ny + YH if gy_count == 2 else ny + 2 * YH
    start = OFF - YH * jnp.minimum(gy, 1) if gy_count == 2 else OFF - YH

    barrier = pltpu.get_barrier_semaphore()
    for other in range(total):
        @pl.when(me != other)
        def _():
            pl.semaphore_signal(
                barrier, inc=1, device_id=(region, other // gy_count, other % gy_count), device_id_type=MESH
            )
    own_rows = pl.ds(OFF, ny)
    own_labels = pl.ds(LH, ny)
    copies = [
        pltpu.make_async_copy(residual, R.at[pl.ds(DEPTH, nz), own_rows], local_sem.at[0]),
        pltpu.make_async_copy(labels, LAB.at[pl.ds(4, nz), own_labels], local_sem.at[1]),
        pltpu.make_async_copy(boundary, BND.at[pl.ds(4, nz), own_labels], local_sem.at[2]),
        pltpu.make_async_copy(iterate, X, local_sem.at[3]),
    ]
    for copy in copies:
        copy.start()
    pl.semaphore_wait(barrier, total - 1)

    steps = (1, -1, 2, -2)

    def target_ok(step):
        return gz + step < gz_count if step > 0 else gz + step >= 0

    def source_ok(step):
        return gz - step >= 0 if step > 0 else gz - step < gz_count

    res_planes = {1: (0, 2, 1), -1: (0, 2, 5), 2: (1, 1, 0), -2: (0, 1, 7)}
    lab_planes = {1: 2, -1: 6, 2: 0, -2: 8}

    def bulk(kind, index, step):
        slot = kind * 4 + index
        if kind == 2:
            first, count, put = res_planes[step]
            src = residual.at[pl.ds(first, count)]
            dst = R.at[pl.ds(put, count), own_rows]
        else:
            src = (labels, boundary)[kind]
            dst = (LAB, BND)[kind].at[pl.ds(lab_planes[step], 2), own_labels]
        return pltpu.make_async_remote_copy(
            src_ref=src, dst_ref=dst, send_sem=bulk_send.at[slot], recv_sem=bulk_recv.at[slot],
            device_id=(region, gz + step, gy), device_id_type=MESH,
        )

    for kind in (0, 1, 2):
        for index, step in enumerate(steps):
            @pl.when(target_ok(step))
            def _():
                bulk(kind, index, step).start()

    def strip(kind, group, side):
        slot = (kind * 5 + group) * 2 + side
        if kind == 2:
            if group == 0:
                put, count = DEPTH, nz
            else:
                _, count, put = res_planes[steps[group - 1]]
            from_row = OFF + ny - YH if side == 0 else OFF
            to_row = OFF - YH if side == 0 else OFF + ny
            size, ref = YH, R
        else:
            put, count = (4, 2) if group == 0 else (lab_planes[steps[group - 1]], 2)
            from_row = ny if side == 0 else LH
            to_row = 0 if side == 0 else LH + ny
            size, ref = LH, (LAB, BND)[kind]
        return pltpu.make_async_remote_copy(
            src_ref=ref.at[pl.ds(put, count), pl.ds(from_row, size)],
            dst_ref=ref.at[pl.ds(put, count), pl.ds(to_row, size)],
            send_sem=strip_send.at[slot], recv_sem=strip_recv.at[slot],
            device_id=(region, gz, gy + (1 if side == 0 else -1)), device_id_type=MESH,
        )

    has_up = gy + 1 < gy_count
    has_down = gy >= 1

    def start_strips(kind, group):
        for side, sends in ((0, has_up), (1, has_down)):
            @pl.when(sends)
            def _():
                strip(kind, group, side).start()

    def finish_strips(kind, group):
        for side, sends, gets in ((0, has_up, has_down), (1, has_down, has_up)):
            @pl.when(gets)
            def _():
                strip(kind, group, side).wait_recv()

            @pl.when(sends)
            def _():
                strip(kind, group, side).wait_send()

    zero_row = jnp.zeros((m, nx), F32)

    def zero_plane(ref, plane):
        def body(j, carry):
            ref[plane, j] = zero_row
            return carry
        lax.fori_loop(0, ny + 2 * OFF, body, 0)

    for index, step in enumerate(steps):
        _, count, put = res_planes[step]

        @pl.when(jnp.logical_not(source_ok(step)))
        def _():
            for plane in range(put, put + count):
                zero_plane(R, plane)
    for plane in range(8):
        for j in list(range(OFF)) + list(range(OFF + ny, 2 * OFF + ny)):
            D[plane, j] = zero_row

    for copy in copies:
        copy.wait()
    for kind in (0, 1, 2):
        start_strips(kind, 0)
    for index, step in enumerate(steps):
        @pl.when(source_ok(step))
        def _():
            for kind in (0, 1):
                bulk(kind, index, step).wait_recv()
                start_strips(kind, 1 + index)
    for kind in (0, 1):
        finish_strips(kind, 0)
    for index, step in enumerate(steps):
        @pl.when(source_ok(step))
        def _():
            for kind in (0, 1):
                finish_strips(kind, 1 + index)

    cell_row = lax.broadcasted_iota(jnp.int32, (ny + 2 * LH, nx), 0)
    cell_col = lax.broadcasted_iota(jnp.int32, (ny + 2 * LH, nx), 1)
    low_row = jnp.where(has_down, 0, LH)
    high_row = jnp.where(has_up, ny + 2 * LH, ny + LH)
    first_plane = 4 - 2 * jnp.minimum(gz, 2)
    last_plane = 6 + 2 * jnp.minimum(gz_count - 1 - gz, 2)

    def coef_body(f, carry):
        there = (cell_row >= jnp.where((f >= first_plane) & (f < last_plane), low_row, ny + 2 * LH)) & (cell_row < high_row)
        coef = jnp.exp(LAB[f].astype(F32) * (contrast_log / (NCLASS - 1)))
        COEF[f] = jnp.where(there, coef, 0.0)
        INNER[f] = jnp.where(there, (1 - BND[f]).astype(F32), 0.0)
        return carry

    lax.fori_loop(0, 10, coef_body, 0)
    rows_cell = ny + 2 * LH

    def field_body(e, carry):
        coef = COEF[e + 1]
        inner = INNER[e + 1]
        diagonal = jnp.zeros_like(coef)
        beside = (
            (WZU, lambda ref: ref[e + 2]),
            (WZD, lambda ref: ref[e]),
            (WYU, lambda ref: pltpu.roll(ref[e + 1], rows_cell - 1, 0)),
            (WYD, lambda ref: pltpu.roll(ref[e + 1], 1, 0)),
            (WXR, lambda ref: jnp.where(cell_col == nx - 1, 0.0, pltpu.roll(ref[e + 1], nx - 1, 1))),
            (WXL, lambda ref: jnp.where(cell_col == 0, 0.0, pltpu.roll(ref[e + 1], 1, 1))),
        )
        for weight, of in beside:
            near = of(COEF)
            face = jnp.where(near > 0.0, 2.0 * coef * near / (coef + near), coef)
            diagonal = diagonal + face
            weight[e] = inner * face * of(INNER)
        diagonal = inner * diagonal + (1.0 - inner)
        DIAG[e] = diagonal
        INV[e] = 1.0 / diagonal
        return carry

    lax.fori_loop(0, 8, field_body, 0)

    def over_rows(first, count, unroll, row):
        def body(i, carry):
            for k in range(unroll):
                row(first + i * unroll + k)
            return carry
        lax.fori_loop(0, count // unroll, body, 0)

    def cell(ref, e, j):
        return ref[e, pl.ds(j + SHIFT, 1), :]

    def scale(planes):
        for e in planes:
            def row(j):
                D[e, j] = cell(INV, e, j) * R[e, j]
            over_rows(start, rows_window, GROUP, row)

    def residual_planes(indices):
        for index in indices:
            @pl.when(source_ok(steps[index]))
            def _():
                bulk(2, index, steps[index]).wait_recv()
                start_strips(2, 1 + index)
        for index in indices:
            @pl.when(source_ok(steps[index]))
            def _():
                finish_strips(2, 1 + index)

    finish_strips(2, 0)
    scale(range(DEPTH, DEPTH + nz))
    residual_planes((0, 1))
    scale((1, 2, 5, 6))

    lane = lax.broadcasted_iota(jnp.int32, (m, 128), 1)
    sub = lax.broadcasted_iota(jnp.int32, (m, 128), 0)

    def place(block, at, to):
        kept = jnp.where((lane >= at) & (lane < at + m), block, 0.0)
        shift = (to - at) % 128
        return pltpu.roll(kept, shift, 1) if shift else kept

    def square(block, at):
        shift = (-at) % 128
        return (pltpu.roll(block, shift, 1) if shift else block)[:, :m]

    def weights(mat_t):
        high = mat_t.astype(BF16).astype(F32)
        rest = mat_t - high
        low = rest.astype(BF16).astype(F32)
        pieces = (high, high, low, high, low, rest - low)
        for i, piece in enumerate(pieces):
            wbuf[:, i * m : (i + 1) * m] = piece
        return wbuf[:, 0 : len(pieces) * m].astype(BF16)

    def mix(left, value):
        high, low = split(value)
        third = (value - high.astype(F32) - low.astype(F32)).astype(BF16)
        pieces = [high, low, high, third, low, high]
        return jnp.dot(left, jnp.concatenate(pieces, axis=0), preferred_element_type=F32)

    own_planes = tuple(range(DEPTH, DEPTH + nz))
    side = GROUP * m

    def gram(pair):
        acc[...] = jnp.zeros_like(acc)
        for e in own_planes:
            def gram_rows(i, carry):
                left, right = pair(e, OFF + i * GROUP)
                left_hi, left_lo = split(left.reshape(side, nx))
                right_hi, right_lo = split(right.reshape(side, nx))
                acc[:, 0:side] += dot_nt(left_hi, right_hi) + (dot_nt(left_hi, right_lo) + dot_nt(left_lo, right_hi))
                return carry
            lax.fori_loop(0, ny // GROUP, gram_rows, 0)
        block = place(acc[0:m, :], 0, 0)
        for i in range(1, GROUP):
            block = block + place(acc[i * m : (i + 1) * m, :], i * m, 0)
        return block

    def residual_pair(e, j):
        res = R[e, pl.ds(j, GROUP)]
        inverse = jnp.stack([jnp.broadcast_to(cell(INV, e, j + k), (m, nx)) for k in range(GROUP)])
        return res, inverse * res

    def direction_pair(e, j):
        return D[e, pl.ds(j, GROUP)], IM[e - 1, pl.ds(j, GROUP)]

    def gram_send_copy(turn, other):
        return pltpu.make_async_remote_copy(
            src_ref=gsend.at[turn], dst_ref=gslots.at[turn, me],
            send_sem=gram_send.at[turn, other], recv_sem=gram_recv.at[turn, me],
            device_id=(region, other // gy_count, other % gy_count), device_id_type=MESH,
        )

    def gram_arrival(turn, other):
        return pltpu.make_async_remote_copy(
            src_ref=gsend.at[turn], dst_ref=gslots.at[turn, other],
            send_sem=gram_send.at[turn, other], recv_sem=gram_recv.at[turn, other],
            device_id=(region, other // gy_count, other % gy_count), device_id_type=MESH,
        )

    def reduce_start(turn, block):
        gsend[turn] = block
        gslots[turn, me] = block
        for other in range(total):
            @pl.when(me != other)
            def _():
                gram_send_copy(turn, other).start()

    def reduce_finish(turn):
        for other in range(total):
            @pl.when(me != other)
            def _():
                gram_arrival(turn, other).wait_recv()
        summed = gslots[turn, 0]
        for other in range(1, total):
            summed = summed + gslots[turn, other]
        for other in range(total):
            @pl.when(me != other)
            def _():
                gram_send_copy(turn, other).wait_send()
        return summed

    def images(planes):
        for e in planes:
            def row(j):
                center = D[e, j]
                coupled = cell(WZU, e, j) * D[e + 1, j] + cell(WZD, e, j) * D[e - 1, j]
                coupled = coupled + cell(WYU, e, j) * D[e, j + 1] + cell(WYD, e, j) * D[e, j - 1]
                coupled = coupled + cell(WXR, e, j) * pltpu.roll(center, nx - 1, 1)
                coupled = coupled + cell(WXL, e, j) * pltpu.roll(center, 1, 1)
                IM[e - 1, j] = cell(DIAG, e, j) * center - coupled
            over_rows(start, rows_window, GROUP, row)

    def residuals(planes, w_step):
        for e in planes:
            def row(j):
                R[e, j] = R[e, j] - mix(w_step, IM[e - 1, j])
            over_rows(start, rows_window, GROUP, row)

    out_it = pltpu.make_async_copy(X, iterate_out, out_sem.at[0])
    out_res = pltpu.make_async_copy(R.at[pl.ds(DEPTH, nz), own_rows], residual_out, out_sem.at[1])
    summed_rho = None
    for it in range(ITERS):
        last = it + 1 == ITERS
        ghosts = [e for e in range(1 + it, 7 - it) if e not in own_planes]
        images(own_planes)
        block = gram(direction_pair)
        if it == 0:
            block = block + pltpu.roll(gram(residual_pair), m, 1)
        reduce_start(2 * it, block)
        if it == 0:
            residual_planes((2, 3))
            scale((0, 7))
        images(ghosts)
        grams = reduce_finish(2 * it)
        if it == 0:
            summed_rho = square(grams, m)
        wbuf[...] = jnp.zeros_like(wbuf)
        wbuf[:, 0:m] = square(grams, 0)
        wbuf[:, m : 2 * m] = summed_rho
        step = square(eliminate(wbuf[...]), m)
        identity = jnp.where(lane == sub, 1.0, 0.0).astype(F32)[:, :m]
        w_step = weights(exact_nt(identity, step))
        residuals(own_planes, w_step)
        if last:
            out_res.start()
        else:
            reduce_start(2 * it + 1, gram(residual_pair))
            residuals(ghosts, w_step)
        for e in own_planes:
            def row(j):
                X[e - DEPTH, j] = X[e - DEPTH, j] + mix(w_step, D[e, j + OFF])
            over_rows(0, ny, GROUP, row)
        if not last:
            wbuf[...] = jnp.where(lane - m == sub, 1.0, 0.0)
            wbuf[:, 0:m] = summed_rho
            inverse_rho = square(eliminate(wbuf[...]), m)
            next_rho = square(reduce_finish(2 * it + 1), 0)
            w_momentum = weights(exact_nt(next_rho, inverse_rho))
            summed_rho = next_rho
            for e in list(own_planes) + ghosts:
                def row(j):
                    D[e, j] = cell(INV, e, j) * R[e, j] + mix(w_momentum, D[e, j])
                over_rows(start, rows_window, GROUP, row)

    out_it.start()
    for kind in (0, 1, 2):
        for index, step in enumerate(steps):
            @pl.when(target_ok(step))
            def _():
                bulk(kind, index, step).wait_send()
    out_it.wait()
    out_res.wait()


def solution(mesh):
    gz_count, gy_count = mesh.shape["gz"], mesh.shape["gy"]
    total = gz_count * gy_count

    def on_device(iterate, residual, labels, boundary):
        m, nz, ny, nx = iterate.shape
        sizes = (gz_count, gy_count, m, nz, ny, nx)
        moved = lambda a: jnp.transpose(a, (1, 2, 0, 3))
        rows, cells = ny + 2 * OFF, ny + 2 * LH
        vmem = lambda *shape: pltpu.VMEM(shape, F32)
        any_spec = pl.BlockSpec(memory_space=pl.ANY)
        shape = jax.ShapeDtypeStruct((nz, ny, m, nx), F32)
        side = GROUP * m
        out = pl.pallas_call(
            functools.partial(kernel, sizes),
            out_shape=(shape, shape),
            in_specs=[any_spec] * 4,
            out_specs=(any_spec, any_spec),
            scratch_shapes=[
                vmem(nz, ny, m, nx), vmem(8, rows, m, nx), vmem(8, rows, m, nx), vmem(6, rows, m, nx),
                pltpu.VMEM((10, cells, nx), jnp.int32), pltpu.VMEM((10, cells, nx), jnp.int32),
                vmem(10, cells, nx), vmem(10, cells, nx),
                *[vmem(8, cells, nx) for _ in range(8)],
                vmem(side, 128), vmem(REDUCES, m, 128), vmem(REDUCES, total, m, 128), vmem(m, 128),
                pltpu.SemaphoreType.DMA((4,)),
                pltpu.SemaphoreType.DMA((12,)), pltpu.SemaphoreType.DMA((12,)),
                pltpu.SemaphoreType.DMA((30,)), pltpu.SemaphoreType.DMA((30,)),
                pltpu.SemaphoreType.DMA((REDUCES, total)), pltpu.SemaphoreType.DMA((REDUCES, total)),
                pltpu.SemaphoreType.DMA((2,)),
            ],
            compiler_params=pltpu.CompilerParams(
                collective_id=0, has_side_effects=True, vmem_limit_bytes=60 * 1024 * 1024
            ),
        )(moved(iterate), moved(residual), labels, boundary)
        back = lambda a: jnp.transpose(a, (2, 0, 1, 3))
        return back(out[0]), back(out[1])

    placed = P(None, ("regions", "gz"), "gy", None)
    cell_placed = P(("regions", "gz"), "gy", None)
    return jax.shard_map(
        on_device,
        mesh=mesh,
        in_specs=(placed, placed, cell_placed, cell_placed),
        out_specs=(placed, placed),
        check_vma=False,
    )
```

time: 469 us -> 270 us (0.58); the launches traced: 463 us -> 270 us
  Pallas kernels: 0 us -> 256 us
  blocking collectives: 186 us -> 0 us
  waiting for transfers between devices: 109 us -> 0 us
  matrix products: 68.6 us -> 0 us
  starting transfers between devices: 39.8 us -> 0 us
  other arithmetic: 33.3 us -> 0 us
  local copies, waits for them, and re-layouts: 24.9 us -> 13.5 us
    pallas_call x0 -> x1, Pallas kernels: none -> 256 us  [on_device(): pl.pallas_call(functools.partial(kernel, sizes), out_shape=(shape, shape)...]
    psum x3 -> x0, blocking collectives: 186 us -> none  [on_device(): lax.psum((gram(residual, scaled), gram(direction, image), gram(scaled, im...]
    ppermute x16 -> x0, waiting for transfers between devices: 109 us -> none  [the longest x8 62.3 us: extended_2(): lax.ppermute(tail, axis, [(i, (i + 1) % count) for i in range(ends)])]
    dot_general x23 -> x0, matrix products: 66.7 us -> none  [the longest x8 38.9 us: combine(): lax.dot_general(weights, flat, (((0,), (0,)), ((), ())), precision=highest)]
    ppermute x16 -> x0, starting transfers between devices: 39.8 us -> none  [the longest x8 28.6 us: extended_2(): lax.ppermute(tail, axis, [(i, (i + 1) % count) for i in range(ends)])]
    another operation x28 -> x0, other arithmetic: 21.8 us -> none  [the longest x15 10.7 us: spd_solve(): factor = jnp.linalg.cholesky(matrix)]
    unnamed x22 -> x4, local copies, waits for them, and re-layouts: 21.5 us -> 6.82 us
    sub x3 -> x0, other arithmetic: 9.72 us -> none  [apply_operator(): return diagonal * center - coupled]
  transfers between devices with their start and end apart: 16 -> 0, of which waited for: 9 -> 0; matrix products, arithmetic and copies ran while one was open for 5% -> 0% of each run, Pallas kernels for 0% -> 0%
where the time goes in v1:
time: 270 us
  Pallas kernels  256 us (95%)
  local copies, waits for them, and re-layouts  13.5 us (5%)
    pallas_call x1, Pallas kernels, on_device(): pl.pallas_call(functools.partial(kernel, sizes), out_shape=(shape, shape)...  256 us
    unnamed x4, local copies, waits for them, and re-layouts  6.82 us
    transpose x1, local copies, waits for them, and re-layouts, on_device(): moved = lambda a: jnp.transpose(a, (1, 2, 0, 3))  6.66 us

profile of v1, /device:TPU:0, one launch (start us, length us, event | category | flops | bytes accessed | tf_op | source)
XLA Modules:
  0.0 269.7 jit_solution(1630122267583136372)
XLA Ops:
  0.6 6.7 %copy_bitcast_fusion = (f32[2,64,16,256]{3,2,1,0:T(8,128)}, f32[2,64,16,256]{3,2,1,0:T(8,128)}) fusion(f32[16,2,64,256]{3,2,1,0:T(8,128)} %param.5, f32[16,2,64,256]{3,2,1,0:T(8,128)} %param.4), kind=kLoop, calls=%fused_computation | loop fusion | bytes 8388608 | tf_op jit(solution)/shard_map/transpose | solution.py:452
  7.3 255.6 %shard_map.59 = (f32[2,64,16,256]{3,2,1,0:T(8,128)}, f32[2,64,16,256]{3,2,1,0:T(8,128)}) custom-call(f32[2,64,16,256]{3,2,1,0:T(8,128)} %get-tuple-element.9.iterate, f32[2,64,16,256]{3,2,1,0:T(8,128)} %get-tuple-element.8.residual, s32[2,64,256]{2,1,0:T(8,128)} %labels.1, s32[2,64,256]{2,1,0:T(8,128)} %boundary.1), custom_call_target="tpu_custom_call" | custom-call | tf_op jit(solution)/shard_map/pallas_call | solution.py:458
  262.9 0.0 copy-start
  262.9 4.3 %copy.8 = f32[16,2,64,256]{3,2,1,0:T(8,128)} copy(f32[16,2,64,256]{3,0,2,1:T(8,128)} %bitcast.7) | data formatting | bytes 4194304
  267.2 0.0 copy-done
  267.2 2.5 copy.9
Async XLA Ops:
  262.9 4.3 %copy-start = (f32[2,64,16,256]{3,2,1,0:T(8,128)S(1)}, f32[2,64,16,256]{3,2,1,0:T(8,128)}, u32[]{:S(2)}) copy-start(f32[2,64,16,256]{3,2,1,0:T(8,128)} %get-tuple-element.5) | copy-start | bytes 6291460

commit v2 on v1

--- a/solution.py
+++ b/solution.py
@@ -16,6 +16,8 @@
 LH = 8
 SHIFT = LH - OFF
 GROUP = 4
+GRAM_GROUPS = 4
+WIDE = 17
 REDUCES = 2 * ITERS - 1
 
 contrast_log = 4.0 * math.log(10.0)
@@ -254,6 +256,8 @@
                 row(first + i * unroll + k)
             return carry
         lax.fori_loop(0, count // unroll, body, 0)
+        for k in range(count // unroll * unroll, count):
+            row(first + k)
 
     def cell(ref, e, j):
         return ref[e, pl.ds(j + SHIFT, 1), :]
@@ -314,12 +318,16 @@
         acc[...] = jnp.zeros_like(acc)
         for e in own_planes:
             def gram_rows(i, carry):
-                left, right = pair(e, OFF + i * GROUP)
-                left_hi, left_lo = split(left.reshape(side, nx))
-                right_hi, right_lo = split(right.reshape(side, nx))
-                acc[:, 0:side] += dot_nt(left_hi, right_hi) + (dot_nt(left_hi, right_lo) + dot_nt(left_lo, right_hi))
+                part = None
+                for k in range(GRAM_GROUPS):
+                    left, right = pair(e, OFF + (i * GRAM_GROUPS + k) * GROUP)
+                    left_hi, left_lo = split(left.reshape(side, nx))
+                    right_hi, right_lo = split(right.reshape(side, nx))
+                    term = dot_nt(left_hi, right_hi) + (dot_nt(left_hi, right_lo) + dot_nt(left_lo, right_hi))
+                    part = term if part is None else part + term
+                acc[:, 0:side] += part
                 return carry
-            lax.fori_loop(0, ny // GROUP, gram_rows, 0)
+            lax.fori_loop(0, ny // (GROUP * GRAM_GROUPS), gram_rows, 0)
         block = place(acc[0:m, :], 0, 0)
         for i in range(1, GROUP):
             block = block + place(acc[i * m : (i + 1) * m, :], i * m, 0)
@@ -378,13 +386,13 @@
                 coupled = coupled + cell(WXR, e, j) * pltpu.roll(center, nx - 1, 1)
                 coupled = coupled + cell(WXL, e, j) * pltpu.roll(center, 1, 1)
                 IM[e - 1, j] = cell(DIAG, e, j) * center - coupled
-            over_rows(start, rows_window, GROUP, row)
+            over_rows(start, rows_window, WIDE, row)
 
     def residuals(planes, w_step):
         for e in planes:
             def row(j):
                 R[e, j] = R[e, j] - mix(w_step, IM[e - 1, j])
-            over_rows(start, rows_window, GROUP, row)
+            over_rows(start, rows_window, WIDE, row)
 
     out_it = pltpu.make_async_copy(X, iterate_out, out_sem.at[0])
     out_res = pltpu.make_async_copy(R.at[pl.ds(DEPTH, nz), own_rows], residual_out, out_sem.at[1])
@@ -419,7 +427,7 @@
         for e in own_planes:
             def row(j):
                 X[e - DEPTH, j] = X[e - DEPTH, j] + mix(w_step, D[e, j + OFF])
-            over_rows(0, ny, GROUP, row)
+            over_rows(0, ny, 4 * GROUP, row)
         if not last:
             wbuf[...] = jnp.where(lane - m == sub, 1.0, 0.0)
             wbuf[:, 0:m] = summed_rho
@@ -430,7 +438,7 @@
             for e in list(own_planes) + ghosts:
                 def row(j):
                     D[e, j] = cell(INV, e, j) * R[e, j] + mix(w_momentum, D[e, j])
-                over_rows(start, rows_window, GROUP, row)
+                over_rows(start, rows_window, WIDE, row)
 
     out_it.start()
     for kind in (0, 1, 2):

time: 270 us -> 198 us (0.73)
  Pallas kernels: 256 us -> 184 us
    pallas_call x1, Pallas kernels: 256 us -> 184 us  [on_device(): pl.pallas_call(functools.partial(kernel, sizes), out_shape=(shape, shape)...]
where the time goes in v2:
time: 198 us
  Pallas kernels  184 us (93%)
  local copies, waits for them, and re-layouts  13.5 us (7%)
    pallas_call x1, Pallas kernels, on_device(): pl.pallas_call(functools.partial(kernel, sizes), out_shape=(shape, shape)...  184 us
    unnamed x4, local copies, waits for them, and re-layouts  6.82 us
    transpose x1, local copies, waits for them, and re-layouts, on_device(): moved = lambda a: jnp.transpose(a, (1, 2, 0, 3))  6.66 us

profile of v2, /device:TPU:0, one launch (start us, length us, event | category | flops | bytes accessed | tf_op | source)
XLA Modules:
  0.0 198.1 jit_solution(12227488356140114795)
XLA Ops:
  0.6 6.7 %copy_bitcast_fusion = (f32[2,64,16,256]{3,2,1,0:T(8,128)}, f32[2,64,16,256]{3,2,1,0:T(8,128)}) fusion(f32[16,2,64,256]{3,2,1,0:T(8,128)} %param.5, f32[16,2,64,256]{3,2,1,0:T(8,128)} %param.4), kind=kLoop, calls=%fused_computation | loop fusion | bytes 8388608 | tf_op jit(solution)/shard_map/transpose | solution.py:460
  7.3 184.0 %shard_map.59 = (f32[2,64,16,256]{3,2,1,0:T(8,128)}, f32[2,64,16,256]{3,2,1,0:T(8,128)}) custom-call(f32[2,64,16,256]{3,2,1,0:T(8,128)} %get-tuple-element.9.iterate, f32[2,64,16,256]{3,2,1,0:T(8,128)} %get-tuple-element.8.residual, s32[2,64,256]{2,1,0:T(8,128)} %labels.1, s32[2,64,256]{2,1,0:T(8,128)} %boundary.1), custom_call_target="tpu_custom_call" | custom-call | tf_op jit(solution)/shard_map/pallas_call | solution.py:466
  191.3 0.0 copy-start
  191.3 4.3 %copy.8 = f32[16,2,64,256]{3,2,1,0:T(8,128)} copy(f32[16,2,64,256]{3,0,2,1:T(8,128)} %bitcast.7) | data formatting | bytes 4194304
  195.6 0.0 copy-done
  195.6 2.5 %copy.9 = f32[16,2,64,256]{3,2,1,0:T(8,128)} copy(f32[16,2,64,256]{3,0,2,1:T(8,128)S(1)} %bitcast.6) | data formatting | bytes 4194304
Async XLA Ops:
  191.3 4.3 %copy-start = (f32[2,64,16,256]{3,2,1,0:T(8,128)S(1)}, f32[2,64,16,256]{3,2,1,0:T(8,128)}, u32[]{:S(2)}) copy-start(f32[2,64,16,256]{3,2,1,0:T(8,128)} %get-tuple-element.5) | copy-start | bytes 6291460
